TPU v7x, 32 devices: a whole 2x2x4 slice. The times are simulated.
32 devices in a mesh: dp: 4 (over y, x), expert: 8 (over z, core).
Axes of the slice: x: 2, y: 2, z: 4, core: 2. Of those that a mesh axis runs over, the one named last changes fastest.
Arguments:
- tokens: bfloat16 [4096, 2048], P(('dp', 'expert')), may hold values from -6 to 6
- expert_ids: int32 [4096, 4], P(('dp', 'expert')), may hold values from 0 to 7, all different within a row; in each aligned block of 128 rows (0 to 127, 128 to 255, ...) at most 80 rows name the same one
- probs: float32 [4096, 4], P(('dp', 'expert')), may hold values from 0.2 to 1
- trade: int32 [4], replicated, may hold values from 0 to 1, as said below
- gate_weight: bfloat16 [8, 2048, 768], P('expert'), may hold values from -0.125 to 0.125
- up_weight: bfloat16 [8, 2048, 768], P('expert'), may hold values from -0.125 to 0.125
- down_weight: bfloat16 [8, 768, 2048], P('expert'), may hold values from -0.21875 to 0.21875
- out_grad: bfloat16 [4096, 2048], P(('dp', 'expert')), may hold values from -0.29882812 to 0.29882812
Outputs:
- combined: bfloat16 [4096, 2048], P(('dp', 'expert'))
- gate_grad: bfloat16 [8, 2048, 768], P('expert', 'dp')
- up_grad: bfloat16 [8, 2048, 768], P('expert', 'dp')
- down_grad: bfloat16 [8, 768, 2048], P('expert', None, 'dp')
Inputs may be any that keep to these rules, and one draw needn't show every extreme that they name: `trade`: index k below 4 pairs expert index k with k + 4; at least one pair trades and at least one does not. `expert_ids`: each row names 4 different experts. Within the 128 rows of one device no expert is named by more than 80 rows, a bound that some block reaches.
All inputs are finite; a program needn't handle non-finite values.
Results may differ from a plain program's by a relative error of at most 0.0095.
Values may be sent and summed in bfloat16 or wider, within the bound.
A program may use at most 128 MiB of HBM per device.

v0:
```python
import jax
import jax.numpy as jnp
from jax import lax
from jax.sharding import PartitionSpec as P


def sparse_local(tokens, expert_ids, probs, trade, gate_weight, up_weight, down_weight, out_grad):
    tok_count, model_width = tokens.shape
    top_count = expert_ids.shape[1]
    hidden_width = gate_weight.shape[2]
    experts = lax.axis_size("expert")
    capacity = 5 * tok_count * top_count // (4 * experts)
    halfway = experts // 2
    chosen = expert_ids.reshape(-1)
    numbers = jnp.arange(experts, dtype=jnp.int32)
    onehot = (chosen[:, None] == numbers[None, :]).astype(jnp.int32)
    earlier = jnp.cumsum(onehot, axis=0) - onehot
    slots = chosen * capacity + jnp.sum(earlier * onehot, axis=1)
    owners = jnp.where(trade[numbers % halfway] == 1, jnp.bitwise_xor(numbers, halfway), numbers)
    pair_tokens = jnp.arange(chosen.shape[0], dtype=jnp.int32) // top_count
    send_rows = (
        jnp.zeros((experts * capacity, model_width), jnp.bfloat16)
        .at[slots]
        .set(tokens[pair_tokens])
    )
    send_rows = send_rows.reshape(experts, capacity, model_width)
    out_pairs = (probs[:, :, None] * out_grad[:, None, :].astype(jnp.float32)).astype(jnp.bfloat16)
    send_grads = (
        jnp.zeros((experts * capacity, model_width), jnp.bfloat16)
        .at[slots]
        .set(out_pairs.reshape(-1, model_width))
    )
    send_grads = send_grads.reshape(experts, capacity, model_width)
    send_rows = send_rows[owners]
    send_grads = send_grads[owners]
    w_gate = gate_weight[0]
    w_up = up_weight[0]
    w_down = down_weight[0]
    arrived = lax.all_to_all(send_rows, "expert", split_axis=0, concat_axis=0, tiled=True)
    lead = arrived.shape[:2]
    flat_rows = arrived.reshape(-1, model_width)
    gate_act = jnp.dot(flat_rows, w_gate, preferred_element_type=jnp.float32)
    up_act = jnp.dot(flat_rows, w_up, preferred_element_type=jnp.float32)
    forward_hidden = (gate_act * jax.nn.sigmoid(gate_act) * up_act).astype(jnp.bfloat16)
    expert_out = jnp.dot(forward_hidden, w_down, preferred_element_type=jnp.float32).astype(
        jnp.bfloat16
    )
    arrived, expert_out, hidden, gate_act, up_act = (
        arrived,
        expert_out.reshape(lead + (model_width,)),
        forward_hidden.reshape(lead + (hidden_width,)),
        gate_act.reshape(lead + (hidden_width,)),
        up_act.reshape(lead + (hidden_width,)),
    )
    returned = lax.all_to_all(expert_out, "expert", split_axis=0, concat_axis=0, tiled=True)
    out_rows = lax.all_to_all(send_grads, "expert", split_axis=0, concat_axis=0, tiled=True)
    returned = returned[owners]
    picked = returned.reshape(-1, model_width)[slots].reshape(tok_count, top_count, model_width)
    combined = jnp.sum(probs[:, :, None] * picked.astype(jnp.float32), axis=1).astype(jnp.bfloat16)
    expert_rows = arrived.reshape(-1, model_width)
    out_rows = out_rows.reshape(-1, model_width)
    hidden = hidden.reshape(-1, hidden_width)
    gate_act = gate_act.reshape(-1, hidden_width)
    up_act = up_act.reshape(-1, hidden_width)
    hidden_grad = lax.dot_general(
        out_rows, w_down, (((1,), (1,)), ((), ())), preferred_element_type=jnp.float32
    )
    sigma = jax.nn.sigmoid(gate_act)
    gate_back = (hidden_grad * up_act * (sigma * (1.0 + gate_act * (1.0 - sigma)))).astype(
        jnp.bfloat16
    )
    up_back = (hidden_grad * (gate_act * sigma)).astype(jnp.bfloat16)
    both_back = jnp.concatenate([gate_back, up_back], axis=1)
    first = lax.dot_general(
        expert_rows, both_back, (((0,), (0,)), ((), ())), preferred_element_type=jnp.float32
    )
    second = lax.dot_general(
        out_rows, hidden, (((0,), (0,)), ((), ())), preferred_element_type=jnp.float32
    )
    summed = lax.psum_scatter(
        jnp.concatenate([first, second], axis=1).astype(jnp.bfloat16),
        "dp",
        scatter_dimension=0,
        tiled=True,
    )
    gate_part = summed[:, :hidden_width]
    up_part = summed[:, hidden_width : 2 * hidden_width]
    down_part = summed[:, 2 * hidden_width :].T
    return (combined, gate_part[None], up_part[None], down_part[None])


def dense_local(tokens, expert_ids, probs, trade, gate_weight, up_weight, down_weight, out_grad):
    hidden_width = gate_weight.shape[2]
    experts = lax.axis_size("expert")
    halfway = experts // 2
    me = lax.axis_index("expert")
    mine = jnp.where(trade[me % halfway] == 1, jnp.bitwise_xor(me, halfway), me)
    rows = lax.all_gather(tokens, "expert", axis=0, tiled=True)
    ids = lax.all_gather(expert_ids, "expert", axis=0, tiled=True)
    weights = lax.all_gather(probs, "expert", axis=0, tiled=True)
    grads = lax.all_gather(out_grad, "expert", axis=0, tiled=True)
    weight = jnp.sum(jnp.where(ids == mine, weights, 0.0), axis=1, keepdims=True)
    w_gate = gate_weight[0]
    w_up = up_weight[0]
    w_down = down_weight[0]
    gate_act = jnp.dot(rows, w_gate, preferred_element_type=jnp.float32)
    up_act = jnp.dot(rows, w_up, preferred_element_type=jnp.float32)
    sigma = jax.nn.sigmoid(gate_act)
    hidden = (gate_act * sigma * up_act).astype(jnp.bfloat16)
    expert_out = jnp.dot(hidden, w_down, preferred_element_type=jnp.float32)
    part = (weight * expert_out).astype(jnp.bfloat16)
    out_rows = (weight * grads.astype(jnp.float32)).astype(jnp.bfloat16)
    hidden_grad = lax.dot_general(
        out_rows, w_down, (((1,), (1,)), ((), ())), preferred_element_type=jnp.float32
    )
    gate_back = (hidden_grad * up_act * (sigma * (1.0 + gate_act * (1.0 - sigma)))).astype(
        jnp.bfloat16
    )
    up_back = (hidden_grad * (gate_act * sigma)).astype(jnp.bfloat16)
    both_back = jnp.concatenate([gate_back, up_back], axis=1)
    first = lax.dot_general(
        rows, both_back, (((0,), (0,)), ((), ())), preferred_element_type=jnp.float32
    )
    second = lax.dot_general(
        out_rows, hidden, (((0,), (0,)), ((), ())), preferred_element_type=jnp.float32
    )
    summed = lax.psum_scatter(
        jnp.concatenate([first, second], axis=1).astype(jnp.bfloat16),
        "dp",
        scatter_dimension=0,
        tiled=True,
    )
    combined = lax.psum_scatter(part, "expert", scatter_dimension=0, tiled=True)
    gate_part = summed[:, :hidden_width]
    up_part = summed[:, hidden_width : 2 * hidden_width]
    down_part = summed[:, 2 * hidden_width :].T
    return (combined, gate_part[None], up_part[None], down_part[None])


def local(tokens, expert_ids, *rest):
    capacity = 5 * tokens.shape[0] * expert_ids.shape[1] // (4 * lax.axis_size("expert"))
    if tokens.shape[0] <= 2 * capacity:
        return dense_local(tokens, expert_ids, *rest)
    return sparse_local(tokens, expert_ids, *rest)


def solution(mesh):
    return jax.shard_map(
        local,
        mesh=mesh,
        in_specs=(
            P(("dp", "expert"), None),
            P(("dp", "expert"), None),
            P(("dp", "expert"), None),
            P(),
            P("expert", None, None),
            P("expert", None, None),
            P("expert", None, None),
            P(("dp", "expert"), None),
        ),
        out_specs=(
            P(("dp", "expert"), None),
            P("expert", "dp", None),
            P("expert", "dp", None),
            P("expert", None, "dp"),
        ),
        check_vma=False,
    )
```

profile of v0, /device:TPU:0, one launch (start us, length us, event | category | flops | bytes accessed | tf_op | source)
XLA Modules:
  0.0 297.5 jit_solution(16371395438921488804)
XLA Ops:
  7.2 0.0 copy-start
  7.2 0.0 all-gather.3.cloned.1.call-start
  7.2 0.7 all-gather.3.cloned.1.call-update
  7.9 0.0 all-gather.5.cloned.1.call-start
  8.0 0.7 all-gather.5.cloned.1.call-update
  8.7 0.0 reduce-scatter.5.cloned.1.call-start
  8.7 1.2 dynamic_slice.3
  10.6 14.7 %all_gather.13 = f32[1024,4]{0,1:T(4,128)S(1)} all-gather(f32[128,4]{0,1:T(4,128)} %param.10), channel_id=1, replica_groups=mesh['dp'=4,'expert'=8] {'expert'}, dimensions={0}, use_global_device_ids=true | all-gather | bytes 18432 | tf_op jit(solution)/shard_map/all_gather | solution.py:100
  25.3 13.3 %all_gather.12 = s32[1024,4]{0,1:T(4,128)S(1)} all-gather(s32[128,4]{0,1:T(4,128)} %param.9), channel_id=1, replica_groups=mesh['dp'=4,'expert'=8] {'expert'}, dimensions={0}, use_global_device_ids=true | all-gather | bytes 18432 | tf_op jit(solution)/shard_map/all_gather | solution.py:99
  38.7 20.7 %all-gather.3.cloned.1.call-done = bf16[1024,2048]{1,0:T(8,128)(2,1)} async-done(((bf16[128,2048]{1,0:T(8,128)(2,1)}), bf16[1024,2048]{1,0:T(8,128)(2,1)}) %all-gather.3.cloned.1.call-update) | async-done | bytes 4194320 | tf_op jit(solution)/shard_map/all_gather | solution.py:98
  59.4 8.3 %fusion.7 = f32[1024,768]{0,1:T(8,128)} fusion(bf16[1024,2048]{1,0:T(8,128)(2,1)} %all-gather.3.cloned.1.call-done, bf16[1,2048,768]{2,1,0:T(8,128)(2,1)} %param.13), kind=kOutput, calls=%fused_computation.12 | convolution fusion | flops 3221225472 | bytes 10485760 | tf_op jit(solution)/shard_map/dot_general | solution.py:107
  67.7 38.9 %all-gather.5.cloned.1.call-done = bf16[1024,2048]{1,0:T(8,128)(2,1)} async-done(((bf16[128,2048]{1,0:T(8,128)(2,1)}), bf16[1024,2048]{1,0:T(8,128)(2,1)}) %all-gather.5.cloned.1.call-update) | async-done | bytes 4194320 | tf_op jit(solution)/shard_map/all_gather | solution.py:101
  106.6 0.0 copy-done
  106.6 0.0 copy-start.1
  106.7 0.0 copy-start.3
  106.7 5.8 %fusion.4 = f32[1024,768]{0,1:T(8,128)S(1)} fusion(bf16[1,768,2048]{2,1,0:T(8,128)(2,1)S(1)} %copy-done, bf16[1024,2048]{1,0:T(8,128)(2,1)} %all-gather.5.cloned.1.call-done, f32[1024]{0:T(1024)S(1)} %select_reduce_fusion), kind=kOutput, calls=%fused_computation.9 | convolution fusion | flops 3227516928 | bytes 10489856 | tf_op jit(solution)/shard_map/dot_general | solution.py:113
  112.5 0.0 copy-done.1
  112.5 0.0 copy-done.3
  112.5 0.0 copy-start.2
  112.5 7.9 %multiply_convert_fusion.3 = (bf16[1024,768]{0,1:T(8,128)(2,1)}, bf16[1024,768]{0,1:T(8,128)(2,1)}, bf16[1024,768]{0,1:T(8,128)(2,1)S(1)}) fusion(f32[1024,768]{0,1:T(8,128)S(1)} %fusion.4, f32[1024,768]{0,1:T(8,128)} %fusion.7, bf16[1024,2048]{1,0:T(8,128)(2,1)S(1)} %copy-done.1, bf16[1,2048,768]{2,1,0:T(8,128)(2,1)S(1)} %copy-done.3), kind=kOutput, calls=%fused_computation.17 | convolution fusion | flops 3233021952 | bytes 18350080 | tf_op jit(solution)/shard_map/dot_general | solution.py:106
  120.4 0.0 copy-start.4
  120.4 0.0 copy-done.2
  120.4 0.0 copy-start.5
  120.4 0.0 copy-start.6
  120.4 3.9 %convolution_convert_fusion.1 = bf16[2048,768]{0,1:T(8,128)(2,1)S(1)} fusion(bf16[1024,768]{0,1:T(8,128)(2,1)S(1)} %get-tuple-element.10, bf16[1024,2048]{1,0:T(8,128)(2,1)S(1)} %copy-done.2, f32[1024]{0:T(1024)S(1)} %select_reduce_fusion), kind=kOutput, calls=%fused_computation.5 | convolution fusion | flops 3229089792 | bytes 8916992 | tf_op jit(solution)/shard_map/dot_general | solution.py:124
  124.3 0.0 copy-done.4
  124.3 0.0 copy-done.5
  124.3 0.0 copy-done.6
  124.3 8.5 %fusion = bf16[2048,1536]{0,1:T(8,128)(2,1)S(1)} fusion(bf16[1024,2048]{1,0:T(8,128)(2,1)S(1)} %copy-done.1, bf16[1024,768]{0,1:T(8,128)(2,1)S(1)} %copy-done.6, bf16[1024,768]{0,1:T(8,128)(2,1)S(1)} %copy-done.5), kind=kOutput, calls=%fused_computation.4 | convolution fusion | flops 6451888128 | bytes 13631488 | tf_op jit(solution)/shard_map/dot_general | solution.py:121
  132.8 11.6 %pad_maximum_fusion = bf16[2048,2304]{0,1:T(8,128)(2,1)} fusion(bf16[2048,768]{0,1:T(8,128)(2,1)S(1)} %convolution_convert_fusion.1, bf16[2048,1536]{0,1:T(8,128)(2,1)S(1)} %fusion), kind=kLoop, calls=%fused_computation | loop fusion | flops 18874368 | bytes 18874368 | tf_op jit(solution)/shard_map/concatenate | solution.py:128
  144.4 0.0 reduce-scatter.5.cloned.1.call-update
  144.5 0.0 reduce-scatter.3.cloned.1.call-start
  144.5 6.7 %multiply_convert_fusion.1 = bf16[1024,2048]{1,0:T(8,128)(2,1)} fusion(bf16[1024,768]{0,1:T(8,128)(2,1)} %copy-done.4, f32[1024]{0:T(1024)S(1)} %select_reduce_fusion, bf16[1,768,2048]{2,1,0:T(8,128)(2,1)S(1)} %copy-done), kind=kOutput, calls=%fused_computation.2 | convolution fusion | flops 3225419776 | bytes 8916992 | tf_op jit(solution)/shard_map/dot_general | solution.py:110
  151.2 0.0 reduce-scatter.3.cloned.1.call-update
  151.3 87.0 %reduce-scatter.5.cloned.1.call-done = bf16[512,2304]{0,1:T(8,128)(2,1)} async-done(((bf16[2048,2304]{0,1:T(8,128)(2,1)}), bf16[512,2304]{0,1:T(8,128)(2,1)}) %reduce-scatter.5.cloned.1.call-update) | async-done | bytes 2359312 | tf_op jit(solution)/shard_map/reduce_scatter | solution.py:127
  238.3 3.1 %slice_bitcast_fusion = (bf16[1,768,512]{2,1,0:T(8,128)(2,1)}, bf16[1,512,768]{1,2,0:T(8,128)(2,1)}, bf16[1,512,768]{1,2,0:T(8,128)(2,1)}) fusion(bf16[512,2304]{0,1:T(8,128)(2,1)} %reduce-scatter.5.cloned.1.call-done), kind=kLoop, calls=%fused_computation.21 | loop fusion | bytes 4718592 | tf_op jit(solution)/shard_map/broadcast_in_dim | solution.py:137
  241.4 2.3 copy.12
  243.7 2.3 copy.13
  245.9 45.0 %reduce-scatter.3.cloned.1.call-done = bf16[128,2048]{1,0:T(8,128)(2,1)} async-done(((bf16[1024,2048]{1,0:T(8,128)(2,1)}), bf16[128,2048]{1,0:T(8,128)(2,1)}) %reduce-scatter.3.cloned.1.call-update) | async-done | bytes 524304 | tf_op jit(solution)/shard_map/reduce_scatter | solution.py:133
  (1 shorter events, 0.0 us)
Async XLA Ops:
  7.2 99.5 %copy-start = (bf16[1,768,2048]{2,1,0:T(8,128)(2,1)S(1)}, bf16[1,768,2048]{2,1,0:T(8,128)(2,1)}, u32[]{:S(2)}) copy-start(bf16[1,768,2048]{2,1,0:T(8,128)(2,1)} %param.14) | copy-start | bytes 9437188
  7.2 52.2 %all-gather.3.cloned.1.call-start = ((), (), s32[]{:S(2)}) async-start(), calls=%async_computation.2 | async-start | bytes 4718592 | tf_op jit(solution)/shard_map/all_gather | solution.py:98
  7.9 98.7 %all-gather.5.cloned.1.call-start = ((), (), s32[]{:S(2)}) async-start(), calls=%async_computation.4 | async-start | bytes 4718592 | tf_op jit(solution)/shard_map/all_gather | solution.py:101
  8.7 229.7 %reduce-scatter.5.cloned.1.call-start = ((), (), s32[]{:S(2)}) async-start(), calls=%async_computation.5 | async-start | bytes 11796480 | tf_op jit(solution)/shard_map/reduce_scatter | solution.py:127
  106.6 5.8 %copy-start.1 = (bf16[1024,2048]{1,0:T(8,128)(2,1)S(1)}, bf16[1024,2048]{1,0:T(8,128)(2,1)}, u32[]{:S(2)}) copy-start(bf16[1024,2048]{1,0:T(8,128)(2,1)} %all-gather.3.cloned.1.call-done) | copy-start | bytes 12582916
  106.7 5.9 %copy-start.3 = (bf16[1,2048,768]{2,1,0:T(8,128)(2,1)S(1)}, bf16[1,2048,768]{2,1,0:T(8,128)(2,1)}, u32[]{:S(2)}) copy-start(bf16[1,2048,768]{2,1,0:T(8,128)(2,1)} %param.12) | copy-start | bytes 9437188
  112.5 7.9 %copy-start.2 = (bf16[1024,2048]{1,0:T(8,128)(2,1)S(1)}, bf16[1024,2048]{1,0:T(8,128)(2,1)}, u32[]{:S(2)}) copy-start(bf16[1024,2048]{1,0:T(8,128)(2,1)} %all-gather.5.cloned.1.call-done) | copy-start | bytes 12582916
  120.4 3.9 %copy-start.4 = (bf16[1024,768]{0,1:T(8,128)(2,1)}, bf16[1024,768]{0,1:T(8,128)(2,1)S(1)}, u32[]{:S(2)}) copy-start(bf16[1024,768]{0,1:T(8,128)(2,1)S(1)} %get-tuple-element.10) | copy-start | bytes 4718596
  120.4 3.9 %copy-start.5 = (bf16[1024,768]{0,1:T(8,128)(2,1)S(1)}, bf16[1024,768]{0,1:T(8,128)(2,1)}, u32[]{:S(2)}) copy-start(bf16[1024,768]{0,1:T(8,128)(2,1)} %get-tuple-element.8) | copy-start | bytes 4718596
  120.4 3.9 %copy-start.6 = (bf16[1024,768]{0,1:T(8,128)(2,1)S(1)}, bf16[1024,768]{0,1:T(8,128)(2,1)}, u32[]{:S(2)}) copy-start(bf16[1024,768]{0,1:T(8,128)(2,1)} %get-tuple-element.9) | copy-start | bytes 4718596
  144.5 146.5 %reduce-scatter.3.cloned.1.call-start = ((), (), s32[]{:S(2)}) async-start(), calls=%async_computation.3 | async-start | bytes 4718592 | tf_op jit(solution)/shard_map/reduce_scatter | solution.py:133
Sparse Core Ops, SparseCore 0:
  9.6 49.7 all-gather.2
  61.0 45.6 all-gather.4
  144.6 93.6 reduce-scatter.4
  241.0 49.8 reduce-scatter.2
where the time goes:
time: 298 us
  waiting for transfers between devices  193 us (65%)
  matrix products  41.2 us (14%)
  blocking collectives  28 us (9%)
  between operations  14.5 us (5%)
  other arithmetic  11.6 us (4%)
  local copies, waits for them, and re-layouts  8.9 us (3%)
    reduce_scatter x1, waiting for transfers between devices, dense_local(): lax.psum_scatter(jnp.concatenate([first, second], axis=1).astype(jnp.bflo...  87 us
    reduce_scatter x1, waiting for transfers between devices, dense_local(): combined = lax.psum_scatter(part, 'expert', scatter_dimension=0, tiled=True)  45 us
    all_gather x1, waiting for transfers between devices, dense_local(): grads = lax.all_gather(out_grad, 'expert', axis=0, tiled=True)  38.9 us
    all_gather x1, waiting for transfers between devices, dense_local(): rows = lax.all_gather(tokens, 'expert', axis=0, tiled=True)  20.7 us
    all_gather x1, blocking collectives, dense_local(): weights = lax.all_gather(probs, 'expert', axis=0, tiled=True)  14.7 us
    all_gather x1, blocking collectives, dense_local(): ids = lax.all_gather(expert_ids, 'expert', axis=0, tiled=True)  13.3 us
    concatenate x1, other arithmetic, dense_local(): jnp.concatenate([first, second], axis=1).astype(jnp.bfloat16)  11.6 us
    dot_general x1, matrix products, dense_local(): lax.dot_general(rows, both_back, (((0,), (0,)), ((), ())), preferred_elem...  8.5 us
  transfers between devices with their start and end apart: 4, of which 4 were waited for; matrix products, arithmetic and copies ran while one was open for 8% of the time, Pallas kernels for 0%

commit v1 on v0

--- a/solution.py
+++ b/solution.py
@@ -98,7 +98,15 @@
     rows = lax.all_gather(tokens, "expert", axis=0, tiled=True)
     ids = lax.all_gather(expert_ids, "expert", axis=0, tiled=True)
     weights = lax.all_gather(probs, "expert", axis=0, tiled=True)
-    grads = lax.all_gather(out_grad, "expert", axis=0, tiled=True)
+    grads = jnp.concatenate(
+        lax.all_to_all(
+            jnp.stack(lax.psum(1, axis_name="expert") * [out_grad], axis=0),
+            axis_name="expert",
+            split_axis=0,
+            concat_axis=0,
+        ),
+        axis=0,
+    )
     weight = jnp.sum(jnp.where(ids == mine, weights, 0.0), axis=1, keepdims=True)
     w_gate = gate_weight[0]
     w_up = up_weight[0]

time: 298 us -> 371 us (1.24)
  blocking collectives: 28 us -> 144 us
  waiting for transfers between devices: 193 us -> 133 us
  other arithmetic: 11.6 us -> 19.4 us
  starting transfers between devices: 0.16 us -> 6.6 us
    all_gather x1, blocking collectives: 14.7 us -> 132 us  [dense_local(): weights = lax.all_gather(probs, 'expert', axis=0, tiled=True)]
    all_gather x1 -> x0, waiting for transfers between devices: 38.9 us -> none  [dense_local(): grads = lax.all_gather(out_grad, 'expert', axis=0, tiled=True)]
    all_gather x1, waiting for transfers between devices: 20.7 us -> 0.01 us  [dense_local(): rows = lax.all_gather(tokens, 'expert', axis=0, tiled=True)]
    convert_element_type x0 -> x2, other arithmetic: none -> 7.81 us  [dense_local(): out_rows = (weight * grads.astype(jnp.float32)).astype(jnp.bfloat16)]
    all_to_all x0 -> x1, starting transfers between devices: none -> 6.49 us  [dense_local(): lax.all_to_all(jnp.stack(lax.psum(1, axis_name='expert') * [out_grad], ax...]
  transfers between devices with their start and end apart: 4 -> 4, of which waited for: 4 -> 2; matrix products, arithmetic and copies ran while one was open for 8% -> 7% of each run, Pallas kernels for 0% -> 0%
where the time goes in v1:
time: 371 us; the launch traced here: 370 us
  blocking collectives  144 us (39%)
  waiting for transfers between devices  133 us (36%)
  matrix products  40.4 us (11%)
  other arithmetic  19.4 us (5%)
  between operations  14.6 us (4%)
  local copies, waits for them, and re-layouts  11.9 us (3%)
  starting transfers between devices  6.6 us (2%)
    all_gather x1, blocking collectives, dense_local(): weights = lax.all_gather(probs, 'expert', axis=0, tiled=True)  132 us
    reduce_scatter x1, waiting for transfers between devices, dense_local(): lax.psum_scatter(jnp.concatenate([first, second], axis=1).astype(jnp.bflo...  87.1 us
    reduce_scatter x1, waiting for transfers between devices, dense_local(): combined = lax.psum_scatter(part, 'expert', scatter_dimension=0, tiled=True)  45.2 us
    all_gather x1, blocking collectives, dense_local(): ids = lax.all_gather(expert_ids, 'expert', axis=0, tiled=True)  12.8 us
    concatenate x1, other arithmetic, dense_local(): jnp.concatenate([first, second], axis=1).astype(jnp.bfloat16)  11.6 us
    dot_general x1, matrix products, dense_local(): lax.dot_general(rows, both_back, (((0,), (0,)), ((), ())), preferred_elem...  8.5 us
    dot_general x1, matrix products, dense_local(): up_act = jnp.dot(rows, w_up, preferred_element_type=jnp.float32)  8.48 us
    dot_general x1, matrix products, dense_local(): gate_act = jnp.dot(rows, w_gate, preferred_element_type=jnp.float32)  8.06 us
  transfers between devices with their start and end apart: 4, of which 2 were waited for; matrix products, arithmetic and copies ran while one was open for 7% of the time, Pallas kernels for 0%

profile of v1, /device:TPU:0, one launch (start us, length us, event | category | flops | bytes accessed | tf_op | source)
XLA Modules:
  0.0 370.4 jit_solution(13234150713163792436)
XLA Ops:
  7.2 0.0 copy-start
  7.2 3.7 stack.2
  10.9 0.0 copy-start.6
  10.9 0.0 copy-start.2
  10.9 0.0 copy-start.3
  10.9 6.5 %all-to-all-start = ((bf16[8,128,2048]{2,1,0:T(8,128)(2,1)}), bf16[8,128,2048]{2,1,0:T(8,128)(2,1)}, u32[]{:S(2)}, u32[]{:S(2)}) async-start(bf16[8,128,2048]{2,1,0:T(8,128)(2,1)} %stack.2), calls=%async_computation.1 | async-start | bytes 8388608 | tf_op jit(solution)/shard_map/all_to_all | solution.py:102
  17.3 0.0 all-gather.2.cloned.1.call-start
  17.4 0.7 all-gather.2.cloned.1.call-update
  18.1 0.0 reduce-scatter.5.cloned.1.call-start
  18.1 0.0 copy-done.6
  18.2 0.6 dynamic_slice.3
  19.4 0.0 copy-done.2
  19.4 131.7 %all_gather.10 = f32[1024,4]{0,1:T(4,128)S(1)} all-gather(f32[128,4]{0,1:T(4,128)S(1)} %copy-done.2), channel_id=1, replica_groups=mesh['dp'=4,'expert'=8] {'expert'}, dimensions={0}, use_global_device_ids=true | all-gather | bytes 18432 | tf_op jit(solution)/shard_map/all_gather | solution.py:100
  151.1 0.0 copy-done.3
  151.1 12.8 %all_gather.9 = s32[1024,4]{0,1:T(4,128)S(1)} all-gather(s32[128,4]{0,1:T(4,128)S(1)} %copy-done.3), channel_id=1, replica_groups=mesh['dp'=4,'expert'=8] {'expert'}, dimensions={0}, use_global_device_ids=true | all-gather | bytes 18432 | tf_op jit(solution)/shard_map/all_gather | solution.py:99
  163.9 0.0 all-to-all-done
  163.9 4.9 %fusion = bf16[1024,2048]{1,0:T(8,128)(2,1)} fusion(f32[1024]{0:T(1024)S(1)} %select_reduce_fusion, bf16[8,128,2048]{2,1,0:T(8,128)(2,1)} %all-to-all-done), kind=kLoop, calls=%fused_computation.2 | loop fusion | flops 6291456 | bytes 8392704 | tf_op jit(solution)/shard_map/convert_element_type | solution.py:120
  168.8 2.9 multiply_convert_fusion
  171.7 0.0 copy-done
  171.7 5.2 %fusion.5 = f32[1024,768]{0,1:T(8,128)} fusion(bf16[1024,2048]{1,0:T(8,128)(2,1)S(1)} %bitcast.37, bf16[1,768,2048]{2,1,0:T(8,128)(2,1)S(1)} %copy-done), kind=kOutput, calls=%fused_computation.11 | convolution fusion | flops 3221225472 | bytes 10485760 | tf_op jit(solution)/shard_map/dot_general | solution.py:121
  176.9 0.0 all-gather.2.cloned.1.call-done
  176.9 0.0 copy-start.4
  176.9 0.0 copy-start.5
  176.9 0.0 copy-start.7
  176.9 8.5 %fusion.8 = f32[1024,768]{0,1:T(8,128)} fusion(bf16[1024,2048]{1,0:T(8,128)(2,1)} %all-gather.2.cloned.1.call-done, bf16[1,2048,768]{2,1,0:T(8,128)(2,1)} %param.13), kind=kOutput, calls=%fused_computation.14 | convolution fusion | flops 3221225472 | bytes 10485760 | tf_op jit(solution)/shard_map/dot_general | solution.py:115
  185.4 0.0 copy-done.4
  185.4 0.0 copy-done.5
  185.4 0.0 copy-done.7
  185.4 0.0 copy-start.1
  185.4 8.1 %multiply_convert_fusion.3 = (bf16[1024,768]{0,1:T(8,128)(2,1)}, bf16[1024,768]{0,1:T(8,128)(2,1)}, bf16[1024,768]{0,1:T(8,128)(2,1)S(1)}) fusion(f32[1024,768]{0,1:T(8,128)S(1)} %copy-done.7, f32[1024,768]{0,1:T(8,128)} %fusion.8, bf16[1024,2048]{1,0:T(8,128)(2,1)S(1)} %copy-done.4, bf16[1,2048,768]{2,1,0:T(8,128)(2,1)S(1)} %copy-done.5), kind=kOutput, calls=%fused_computation.19 | convolution fusion | flops 3233021952 | bytes 18350080 | tf_op jit(solution)/shard_map/dot_general | solution.py:114
  193.5 0.0 copy-done.1
  193.5 0.0 copy-start.9
  193.5 0.0 copy-start.10
  193.5 3.6 convolution_convert_fusion.1
  197.2 0.0 copy-done.8
  197.2 0.0 copy-done.9
  197.2 0.0 copy-done.10
  197.2 8.5 %fusion.1 = bf16[2048,1536]{0,1:T(8,128)(2,1)S(1)} fusion(bf16[1024,2048]{1,0:T(8,128)(2,1)S(1)} %copy-done.4, bf16[1024,768]{0,1:T(8,128)(2,1)S(1)} %copy-done.10, bf16[1024,768]{0,1:T(8,128)(2,1)S(1)} %copy-done.9), kind=kOutput, calls=%fused_computation.6 | convolution fusion | flops 6451888128 | bytes 13631488 | tf_op jit(solution)/shard_map/dot_general | solution.py:129
  205.7 11.6 %pad_maximum_fusion = bf16[2048,2304]{0,1:T(8,128)(2,1)} fusion(bf16[2048,768]{0,1:T(8,128)(2,1)S(1)} %convolution_convert_fusion.1, bf16[2048,1536]{0,1:T(8,128)(2,1)S(1)} %fusion.1), kind=kLoop, calls=%fused_computation | loop fusion | flops 18874368 | bytes 18874368 | tf_op jit(solution)/shard_map/concatenate | solution.py:136
  217.3 0.0 reduce-scatter.5.cloned.1.call-update
  217.3 0.0 reduce-scatter.3.cloned.1.call-start
  217.4 6.5 %multiply_convert_fusion.1 = bf16[1024,2048]{1,0:T(8,128)(2,1)} fusion(bf16[1024,768]{0,1:T(8,128)(2,1)} %copy-done.8, f32[1024]{0:T(1024)S(1)} %select_reduce_fusion, bf16[1,768,2048]{2,1,0:T(8,128)(2,1)S(1)} %copy-done), kind=kOutput, calls=%fused_computation.4 | convolution fusion | flops 3225419776 | bytes 8916992 | tf_op jit(solution)/shard_map/dot_general | solution.py:118
  223.9 0.0 reduce-scatter.3.cloned.1.call-update
  223.9 87.1 %reduce-scatter.5.cloned.1.call-done = bf16[512,2304]{0,1:T(8,128)(2,1)} async-done(((bf16[2048,2304]{0,1:T(8,128)(2,1)}), bf16[512,2304]{0,1:T(8,128)(2,1)}) %reduce-scatter.5.cloned.1.call-update) | async-done | bytes 2359312 | tf_op jit(solution)/shard_map/reduce_scatter | solution.py:135
  311.0 3.1 slice_bitcast_fusion
  314.1 2.3 copy.12
  316.3 2.3 copy.13
  318.6 45.2 %reduce-scatter.3.cloned.1.call-done = bf16[128,2048]{1,0:T(8,128)(2,1)} async-done(((bf16[1024,2048]{1,0:T(8,128)(2,1)}), bf16[128,2048]{1,0:T(8,128)(2,1)}) %reduce-scatter.3.cloned.1.call-update) | async-done | bytes 524304 | tf_op jit(solution)/shard_map/reduce_scatter | solution.py:141
  (2 shorter events, 0.0 us)
Async XLA Ops:
  7.2 164.6 %copy-start = (bf16[1,768,2048]{2,1,0:T(8,128)(2,1)S(1)}, bf16[1,768,2048]{2,1,0:T(8,128)(2,1)}, u32[]{:S(2)}) copy-start(bf16[1,768,2048]{2,1,0:T(8,128)(2,1)} %param.14) | copy-start | bytes 9437188
  10.9 7.3 %copy-start.6 = (s32[4]{0:T(128)S(1)}, s32[4]{0:T(128)}, u32[]{:S(2)}) copy-start(s32[4]{0:T(128)} %param.11) | copy-start | bytes 52
  10.9 8.5 %copy-start.2 = (f32[128,4]{0,1:T(4,128)S(1)}, f32[128,4]{0,1:T(4,128)}, u32[]{:S(2)}) copy-start(f32[128,4]{0,1:T(4,128)} %param.10) | copy-start | bytes 6148
  10.9 140.3 %copy-start.3 = (s32[128,4]{0,1:T(4,128)S(1)}, s32[128,4]{0,1:T(4,128)}, u32[]{:S(2)}) copy-start(s32[128,4]{0,1:T(4,128)} %param.9) | copy-start | bytes 6148
  10.9 153.0 %all-to-all-start = ((bf16[8,128,2048]{2,1,0:T(8,128)(2,1)}), bf16[8,128,2048]{2,1,0:T(8,128)(2,1)}, u32[]{:S(2)}, u32[]{:S(2)}) async-start(bf16[8,128,2048]{2,1,0:T(8,128)(2,1)} %stack.2), calls=%async_computation.1 | async-start | bytes 8388608 | tf_op jit(solution)/shard_map/all_to_all | solution.py:102
  17.3 159.6 %all-gather.2.cloned.1.call-start = ((), (), s32[]{:S(2)}) async-start(), calls=%async_computation.3 | async-start | bytes 4718592 | tf_op jit(solution)/shard_map/all_gather | solution.py:98
  18.1 292.9 %reduce-scatter.5.cloned.1.call-start = ((), (), s32[]{:S(2)}) async-start(), calls=%async_computation.5 | async-start | bytes 11796480 | tf_op jit(solution)/shard_map/reduce_scatter | solution.py:135
  176.9 8.5 %copy-start.4 = (bf16[1024,2048]{1,0:T(8,128)(2,1)S(1)}, bf16[1024,2048]{1,0:T(8,128)(2,1)}, u32[]{:S(2)}) copy-start(bf16[1024,2048]{1,0:T(8,128)(2,1)} %all-gather.2.cloned.1.call-done) | copy-start | bytes 12582916
  176.9 8.5 %copy-start.5 = (bf16[1,2048,768]{2,1,0:T(8,128)(2,1)S(1)}, bf16[1,2048,768]{2,1,0:T(8,128)(2,1)}, u32[]{:S(2)}) copy-start(bf16[1,2048,768]{2,1,0:T(8,128)(2,1)} %param.12) | copy-start | bytes 9437188
  176.9 8.5 %copy-start.7 = (f32[1024,768]{0,1:T(8,128)S(1)}, f32[1024,768]{0,1:T(8,128)}, u32[]{:S(2)}) copy-start(f32[1024,768]{0,1:T(8,128)} %fusion.5) | copy-start | bytes 9437188
  185.4 8.1 %copy-start.1 = (bf16[1024,2048]{1,0:T(8,128)(2,1)S(1)}, bf16[1024,2048]{1,0:T(8,128)(2,1)}, u32[]{:S(2)}) copy-start(bf16[1024,2048]{1,0:T(8,128)(2,1)} %fusion) | copy-start | bytes 12582916
  193.5 3.7 copy-start.8
  193.5 3.7 copy-start.9
  193.5 3.7 copy-start.10
  217.3 146.5 %reduce-scatter.3.cloned.1.call-start = ((), (), s32[]{:S(2)}) async-start(), calls=%async_computation.4 | async-start | bytes 4718592 | tf_op jit(solution)/shard_map/reduce_scatter | solution.py:141
Sparse Core Ops, SparseCore 0:
  19.8 81.5 all-gather.1
  217.5 93.4 reduce-scatter.4
  313.9 49.8 reduce-scatter.2
